TPU v7x, 32 devices: a whole 2x2x4 slice. The times are simulated.
32 devices in a mesh: grp: 2 (over y), row: 4 (over z), col: 4 (over x, core).
Axes of the slice: x: 2, y: 2, z: 4, core: 2. Of those that a mesh axis runs over, the one named last changes fastest.
Arguments:
- inputs: bfloat16 [256, 16384], P(('grp', 'row'), 'col'), parts along dimension 0, may hold values from -6 to 6
- output_gradient: bfloat16 [256, 16384], P(('grp', 'row'), 'col'), parts along dimension 0, may hold values from -6 to 6
- gate_preactivation: bfloat16 [256, 8192], P('grp', 'row'), parts along dimension 0, may hold values from -6 to 6
- up_preactivation: bfloat16 [256, 8192], P('grp', 'row'), parts along dimension 0, may hold values from -6 to 6
- gate_weight: bfloat16 [16384, 8192], P('col', 'row'), may hold values from -0.046875 to 0.046875
- up_weight: bfloat16 [16384, 8192], P('col', 'row'), may hold values from -0.046875 to 0.046875
- down_weight: bfloat16 [8192, 16384], P('row', 'col'), may hold values from -0.0625 to 0.0625
- up_adapter_entry: bfloat16 [16, 16384], P(None, 'col'), may hold values from -6 to 6
- up_adapter_exit: bfloat16 [16, 8192], P(None, 'row'), may hold values from -0.0032958984 to 0.0032958984
- down_adapter_entry: bfloat16 [16, 8192], P(None, 'row'), may hold values from -6 to 6
- down_adapter_exit: bfloat16 [16, 16384], P(None, 'col'), may hold values from -0.0023956299 to 0.0023956299
- up_adapter_activations: bfloat16 [16, 256], P(None, 'grp'), parts along dimension 1, may hold values from -0.29882812 to 0.29882812
- down_adapter_activations: bfloat16 [16, 256], P(None, 'grp'), parts along dimension 1, may hold values from -0.29882812 to 0.29882812
Outputs:
- grad_inputs: bfloat16 [256, 16384], P(('grp', 'row'), 'col'), parts along dimension 0
- up_entry_gradient: float32 [32, 16384], P('grp', 'col'), parts along dimension 0
- up_exit_gradient: float32 [32, 8192], P('grp', 'row'), parts along dimension 0
- down_entry_gradient: float32 [32, 8192], P('grp', 'row'), parts along dimension 0
- down_exit_gradient: float32 [32, 16384], P('grp', 'col'), parts along dimension 0
There are 2 independent parts, one for each index of `grp`. A program takes and returns all parts, laid end to end along the dimension named above; an argument that names none is the same for every part. Nothing has to cross between parts.
All inputs are finite; a program needn't handle non-finite values.
Results may differ from a plain program's by a relative error of at most 0.005.
Values may be sent and summed in bfloat16 or wider, within the bound.
No kernel may reach another device: no remote copies, remote signals or barrier semaphores. Data moves between devices by JAX's collectives and lax.ppermute only.
A program may use at most 128 MiB of HBM per device.

v0:
```python
import jax
import jax.numpy as jnp
from jax import lax
from jax.sharding import PartitionSpec as P

adapter_scale = 2.0


def contract_trailing(left, right):
    return lax.dot_general(
        left, right, (((1,), (1,)), ((), ())), preferred_element_type=jnp.float32
    )


def contract_leading(left, right, matmul_accuracy=None):
    return lax.dot_general(
        left,
        right,
        (((0,), (0,)), ((), ())),
        precision=matmul_accuracy,
        preferred_element_type=jnp.float32,
    )


def body(
    inputs,
    output_gradient,
    gate_preactivation,
    up_preactivation,
    gate_weight,
    up_weight,
    down_weight,
    up_adapter_entry,
    up_adapter_exit,
    down_adapter_entry,
    down_adapter_exit,
    up_adapter_activations,
    down_adapter_activations,
):
    highest_setting = lax.Precision.HIGHEST
    complete_gradient = lax.all_gather(output_gradient, "row", axis=0, tiled=True)
    down_piece = contract_trailing(complete_gradient, down_adapter_exit)
    hidden_piece = contract_trailing(complete_gradient, down_weight)
    hidden_piece = hidden_piece + adapter_scale * jnp.dot(
        down_piece, down_adapter_entry.astype(jnp.float32), precision=highest_setting
    )
    hidden_gradient, down_full = lax.psum((hidden_piece, down_piece), "col")
    gate_f = gate_preactivation.astype(jnp.float32)
    up_f = up_preactivation.astype(jnp.float32)
    sigmoid_gate = jax.nn.sigmoid(gate_f)
    hidden_state = (gate_f * sigmoid_gate * up_f).astype(jnp.bfloat16)
    gate_grad = (
        hidden_gradient * up_f * sigmoid_gate * (1.0 + gate_f * (1.0 - sigmoid_gate))
    ).astype(jnp.bfloat16)
    up_gradient = (hidden_gradient * gate_f * sigmoid_gate).astype(jnp.bfloat16)
    down_rounded_value = down_full.astype(jnp.bfloat16)
    upper_piece = contract_trailing(up_gradient, up_adapter_exit)
    input_piece = contract_trailing(gate_grad, gate_weight) + contract_trailing(
        up_gradient, up_weight
    )
    input_piece = input_piece + adapter_scale * jnp.dot(
        upper_piece, up_adapter_entry.astype(jnp.float32), precision=highest_setting
    )
    input_grad, upper_full = (
        lax.psum_scatter(input_piece, "row", scatter_dimension=0, tiled=True),
        lax.psum_scatter(upper_piece, "row", scatter_dimension=0, tiled=True),
    )
    up_entry_term = adapter_scale * contract_leading(
        upper_full, inputs.astype(jnp.float32), matmul_accuracy=highest_setting
    )
    up_entry_gradient = lax.psum(up_entry_term, "row")
    up_exit_gradient = adapter_scale * jnp.dot(
        up_adapter_activations, up_gradient, preferred_element_type=jnp.float32
    )
    down_entry_gradient = adapter_scale * contract_leading(down_rounded_value, hidden_state)
    down_exit_gradient = adapter_scale * jnp.dot(
        down_adapter_activations, complete_gradient, preferred_element_type=jnp.float32
    )
    return (
        input_grad.astype(jnp.bfloat16),
        up_entry_gradient,
        up_exit_gradient,
        down_entry_gradient,
        down_exit_gradient,
    )


def solution(mesh):
    placed = (
        P(("grp", "row"), "col"),
        P(("grp", "row"), "col"),
        P("grp", "row"),
        P("grp", "row"),
        P("col", "row"),
        P("col", "row"),
        P("row", "col"),
        P(None, "col"),
        P(None, "row"),
        P(None, "row"),
        P(None, "col"),
        P(None, "grp"),
        P(None, "grp"),
    )
    return jax.shard_map(
        body,
        mesh=mesh,
        in_specs=placed,
        out_specs=(
            P(("grp", "row"), "col"),
            P("grp", "col"),
            P("grp", "row"),
            P("grp", "row"),
            P("grp", "col"),
        ),
        check_vma=False,
    )
```

profile of v0, /device:TPU:0, one launch (start us, length us, event | category | flops | bytes accessed | tf_op | source)
XLA Modules:
  0.0 212.7 jit_solution(2744428697788110122)
XLA Ops:
  7.3 0.7 all-gather.2.cloned.1.call-update
  8.0 32.3 %all-gather.2.cloned.1.call-done = bf16[128,4096]{1,0:T(8,128)(2,1)} async-done(((bf16[32,4096]{1,0:T(8,128)(2,1)}), bf16[128,4096]{1,0:T(8,128)(2,1)}) %all-gather.2.cloned.1.call-update) | async-done | bytes 1048592 | tf_op jit(solution)/shard_map/all_gather | solution.py:41
  40.3 1.6 fusion.21
  41.9 11.8 %fusion.20 = f32[128,2048]{1,0:T(8,128)S(1)} fusion(bf16[128,4096]{1,0:T(8,128)(2,1)} %all-gather.2.cloned.1.call-done, bf16[2048,4096]{1,0:T(8,128)(2,1)} %param.19), kind=kOutput, calls=%fused_computation.31 | convolution fusion | flops 2147483648 | bytes 18874368 | tf_op jit(solution)/shard_map/dot_general | solution.py:10
  53.7 1.6 fusion.1
  55.3 35.7 %all-reduce.3.cloned.1.call-done = f32[128,2048]{1,0:T(8,128)} async-done(((f32[128,2048]{1,0:T(8,128)}), f32[128,2048]{1,0:T(8,128)}) %all-reduce.3.cloned.1.call-update) | async-done | bytes 1048592 | tf_op jit(solution)/shard_map/psum | solution.py:47
  91.0 1.5 fusion.12
  92.5 0.8 copy-done.2
  93.3 0.2 fusion.22
  93.6 0.8 copy.18
  94.4 0.2 reduce-scatter.5.cloned.1.call-start
  94.6 13.2 %fusion.13 = f32[128,4096]{1,0:T(8,128)} fusion(bf16[4096,2048]{1,0:T(8,128)(2,1)} %param.17, f32[128,2048]{1,0:T(8,128)} %all-reduce.3.cloned.1.call-done, bf16[128,2048]{1,0:T(8,128)(2,1)S(1)} %copy-done.7, bf16[128,2048]{1,0:T(8,128)(2,1)S(1)} %copy-done.3), kind=kOutput, calls=%fused_computation.26 | convolution fusion | flops 2150629376 | bytes 20971520 | tf_op jit(solution)/shard_map/dot_general | solution.py:10
  107.8 12.3 %convolution_add_fusion = f32[128,4096]{1,0:T(8,128)S(1)} fusion(f32[128,4096]{1,0:T(8,128)} %fusion.13, bf16[128,2048]{1,0:T(8,128)(2,1)} %copy-done.2, bf16[4096,2048]{1,0:T(8,128)(2,1)} %param.18), kind=kOutput, calls=%fused_computation.2 | convolution fusion | flops 2148007936 | bytes 21495808 | tf_op jit(solution)/shard_map/dot_general | solution.py:10
  120.1 2.4 %fusion = f32[128,4096]{1,0:T(8,128)} fusion(f32[128,4096]{1,0:T(8,128)S(1)} %convolution_add_fusion, f32[128,16]{0,1:T(8,128)S(1)} %fusion.22, bf16[16,4096]{1,0:T(8,128)(2,1)S(1)} %copy-done.4), kind=kOutput, calls=%fused_computation.1 | convolution fusion | flops 101711872 | bytes 4333568 | tf_op jit(solution)/shard_map/dot_general | solution.py:61
  122.5 0.0 all-reduce.5.cloned.1.call-start
  122.6 6.0 %psum.23 = bf16[128,16]{0,1:T(8,128)(2,1)S(1)} all-reduce(f32[128,16]{0,1:T(8,128)S(1)} %fusion.21), channel_id=1, replica_groups=mesh['grp'=2,'row'=4,'col'=4] {'col'}, use_global_device_ids=true, to_apply=%region_4.0 | all-reduce | flops 2048 | bytes 12288 | tf_op jit(solution)/shard_map/psum | solution.py:47
  128.6 2.4 %convolution_multiply_fusion.5 = f32[16,2048]{1,0:T(8,128)} fusion(bf16[128,2048]{1,0:T(8,128)(2,1)} %param.16, bf16[128,2048]{1,0:T(8,128)(2,1)} %param.15, bf16[128,16]{0,1:T(8,128)(2,1)S(1)} %psum.23), kind=kOutput, calls=%fused_computation.9 | convolution fusion | flops 10518528 | bytes 1183744 | tf_op jit(solution)/shard_map/dot_general | solution.py:16
  131.0 1.7 convolution_multiply_fusion.2
  132.8 1.6 convolution_multiply_fusion.1
  134.4 1.9 fusion.2
  136.3 30.6 %reduce-scatter.5.cloned.1.call-done = f32[32,4096]{1,0:T(8,128)} async-done(((f32[128,4096]{1,0:T(8,128)}), f32[32,4096]{1,0:T(8,128)}) %reduce-scatter.5.cloned.1.call-update) | async-done | bytes 524304 | tf_op jit(solution)/shard_map/reduce_scatter | solution.py:65
  166.9 1.8 convert_element_type.28
  168.7 35.8 %all-reduce.5.cloned.1.call-done = f32[16,4096]{1,0:T(8,128)} async-done(((f32[16,4096]{1,0:T(8,128)}), f32[16,4096]{1,0:T(8,128)}) %all-reduce.5.cloned.1.call-update) | async-done | bytes 262160 | tf_op jit(solution)/shard_map/psum | solution.py:71
  204.5 1.7 copy.22
  (23 shorter events, 0.2 us)
Async XLA Ops:
  7.2 123.8 %copy-start = (bf16[32,4096]{1,0:T(8,128)(2,1)S(1)}, bf16[32,4096]{1,0:T(8,128)(2,1)}, u32[]{:S(2)}) copy-start(bf16[32,4096]{1,0:T(8,128)(2,1)} %param.13) | copy-start | bytes 786436
  7.2 46.5 %copy-start.5 = (bf16[16,2048]{1,0:T(8,128)(2,1)S(1)}, bf16[16,2048]{1,0:T(8,128)(2,1)}, u32[]{:S(2)}) copy-start(bf16[16,2048]{1,0:T(8,128)(2,1)} %param.22) | copy-start | bytes 196612
  7.2 83.8 %copy-start.3 = (bf16[128,2048]{1,0:T(8,128)(2,1)S(1)}, bf16[128,2048]{1,0:T(8,128)(2,1)}, u32[]{:S(2)}) copy-start(bf16[128,2048]{1,0:T(8,128)(2,1)} %param.15) | copy-start | bytes 1572868
  7.2 86.1 %copy-start.6 = (bf16[16,2048]{1,0:T(8,128)(2,1)S(1)}, bf16[16,2048]{1,0:T(8,128)(2,1)}, u32[]{:S(2)}) copy-start(bf16[16,2048]{1,0:T(8,128)(2,1)} %param.21) | copy-start | bytes 196612
  7.2 87.4 %copy-start.7 = (bf16[128,2048]{1,0:T(8,128)(2,1)S(1)}, bf16[128,2048]{1,0:T(8,128)(2,1)}, u32[]{:S(2)}) copy-start(bf16[128,2048]{1,0:T(8,128)(2,1)} %param.16) | copy-start | bytes 1572868
  7.2 33.1 %all-gather.2.cloned.1.call-start = ((), (), s32[]{:S(2)}) async-start(), calls=%async_computation.2 | async-start | bytes 1310720 | tf_op jit(solution)/shard_map/all_gather | solution.py:41
  8.0 83.1 %all-reduce.3.cloned.1.call-start = ((), (), s32[]{:S(2)}) async-start(), calls=%async_computation.3 | async-start | bytes 2097152 | tf_op jit(solution)/shard_map/psum | solution.py:47
  55.3 75.7 %reduce-scatter.7.cloned.1.call-start = ((), (), s32[]{:S(2)}) async-start(), calls=%async_computation.6 | async-start | bytes 81920
  92.5 0.8 copy-start.2
  94.4 25.7 %copy-start.4 = (bf16[16,4096]{1,0:T(8,128)(2,1)S(1)}, bf16[16,4096]{1,0:T(8,128)(2,1)}, u32[]{:S(2)}) copy-start(bf16[16,4096]{1,0:T(8,128)(2,1)} %param.20) | copy-start | bytes 393220
  94.4 72.5 %reduce-scatter.5.cloned.1.call-start = ((), (), s32[]{:S(2)}) async-start(), calls=%async_computation.4 | async-start | bytes 2621440 | tf_op jit(solution)/shard_map/reduce_scatter | solution.py:65
  107.8 25.0 %copy-start.1 = (bf16[128,4096]{1,0:T(8,128)(2,1)S(1)}, bf16[128,4096]{1,0:T(8,128)(2,1)}, u32[]{:S(2)}) copy-start(bf16[128,4096]{1,0:T(8,128)(2,1)} %all-gather.2.cloned.1.call-done) | copy-start | bytes 3145732
  122.5 82.0 %all-reduce.5.cloned.1.call-start = ((), (), s32[]{:S(2)}) async-start(), calls=%async_computation.5 | async-start | bytes 524288 | tf_op jit(solution)/shard_map/psum | solution.py:71
Sparse Core Ops, SparseCore 0:
  9.6 30.6 all-gather.1
  55.4 35.5 all-reduce.2
  94.5 19.4 reduce-scatter.6
  122.6 44.2 reduce-scatter.4
  169.8 34.6 all-reduce.4
where the time goes:
time: 213 us
  waiting for transfers between devices  135 us (63%)
  matrix products  50.8 us (24%)
  between operations  13.9 us (7%)
  blocking collectives  6 us (3%)
  other arithmetic  3.28 us (2%)
  local copies, waits for them, and re-layouts  3.27 us (2%)
    dot_general x5, matrix products, contract_trailing(): lax.dot_general(left, right, (((1,), (1,)), ((), ())), preferred_element_...  39 us
    psum x1, waiting for transfers between devices, body(): up_entry_gradient = lax.psum(up_entry_term, 'row')  35.8 us
    psum x1, waiting for transfers between devices, body(): hidden_gradient, down_full = lax.psum((hidden_piece, down_piece), 'col')  35.7 us
    all_gather x1, waiting for transfers between devices, body(): lax.all_gather(output_gradient, 'row', axis=0, tiled=True)  32.3 us
    reduce_scatter x1, waiting for transfers between devices, body(): lax.psum_scatter(input_piece, 'row', scatter_dimension=0, tiled=True)  30.6 us
    psum x1, blocking collectives, body(): hidden_gradient, down_full = lax.psum((hidden_piece, down_piece), 'col')  6 us
  transfers between devices with their start and end apart: 5, of which 4 were waited for; matrix products, arithmetic and copies ran while one was open for 18% of the time, Pallas kernels for 0%

commit v1 on v0

--- a/solution.py
+++ b/solution.py
@@ -68,7 +68,7 @@
     up_entry_term = adapter_scale * contract_leading(
         upper_full, inputs.astype(jnp.float32), matmul_accuracy=highest_setting
     )
-    up_entry_gradient = lax.psum(up_entry_term, "row")
+    up_entry_gradient = jnp.sum(lax.all_gather(up_entry_term, "row"), axis=0)
     up_exit_gradient = adapter_scale * jnp.dot(
         up_adapter_activations, up_gradient, preferred_element_type=jnp.float32
     )

time: 213 us -> 196 us (0.920)
  waiting for transfers between devices: 135 us -> 118 us
    psum x1 -> x0, waiting for transfers between devices: 35.8 us -> none  [body(): up_entry_gradient = lax.psum(up_entry_term, 'row')]
    unnamed x6, waiting for transfers between devices: 0.75 us -> 20.3 us
where the time goes in v1:
time: 196 us
  waiting for transfers between devices  118 us (60%)
  matrix products  50.9 us (26%)
  between operations  13.9 us (7%)
  blocking collectives  5.76 us (3%)
  other arithmetic  5.3 us (3%)
    dot_general x5, matrix products, contract_trailing(): lax.dot_general(left, right, (((1,), (1,)), ((), ())), preferred_element_...  39.3 us
    psum x1, waiting for transfers between devices, body(): hidden_gradient, down_full = lax.psum((hidden_piece, down_piece), 'col')  35.7 us
    all_gather x1, waiting for transfers between devices, body(): lax.all_gather(output_gradient, 'row', axis=0, tiled=True)  32.3 us
    reduce_scatter x1, waiting for transfers between devices, body(): lax.psum_scatter(input_piece, 'row', scatter_dimension=0, tiled=True)  29.9 us
    unnamed x6, waiting for transfers between devices  20.3 us
    psum x1, blocking collectives, body(): hidden_gradient, down_full = lax.psum((hidden_piece, down_piece), 'col')  5.76 us
    dot_general x2, matrix products, contract_leading(): lax.dot_general(left, right, (((0,), (0,)), ((), ())), precision=matmul_a...  4.02 us
  transfers between devices with their start and end apart: 5, of which 4 were waited for; matrix products, arithmetic and copies ran while one was open for 18% of the time, Pallas kernels for 0%

profile of v1, /device:TPU:0, one launch (start us, length us, event | category | flops | bytes accessed | tf_op | source)
XLA Modules:
  0.0 195.9 jit_solution(463190421693803917)
XLA Ops:
  7.3 0.7 all-gather.4.cloned.1.call-update
  8.0 32.3 %all-gather.4.cloned.1.call-done = bf16[128,4096]{1,0:T(8,128)(2,1)} async-done(((bf16[32,4096]{1,0:T(8,128)(2,1)}), bf16[128,4096]{1,0:T(8,128)(2,1)}) %all-gather.4.cloned.1.call-update) | async-done | bytes 1048592 | tf_op jit(solution)/shard_map/all_gather | solution.py:41
  40.3 1.6 fusion.21
  41.9 11.8 %fusion.20 = f32[128,2048]{1,0:T(8,128)S(1)} fusion(bf16[128,4096]{1,0:T(8,128)(2,1)} %all-gather.4.cloned.1.call-done, bf16[2048,4096]{1,0:T(8,128)(2,1)} %param.19), kind=kOutput, calls=%fused_computation.31 | convolution fusion | flops 2147483648 | bytes 18874368 | tf_op jit(solution)/shard_map/dot_general | solution.py:10
  53.7 1.6 fusion.1
  55.3 0.0 reduce-scatter.7.cloned.1.call-start
  55.4 35.7 %all-reduce.2.cloned.1.call-done = f32[128,2048]{1,0:T(8,128)} async-done(((f32[128,2048]{1,0:T(8,128)}), f32[128,2048]{1,0:T(8,128)}) %all-reduce.2.cloned.1.call-update) | async-done | bytes 1048592 | tf_op jit(solution)/shard_map/psum | solution.py:47
  91.0 1.5 fusion.12
  92.5 0.8 copy-done.2
  93.4 0.2 fusion.22
  93.6 0.8 copy.18
  94.4 19.5 %reduce-scatter.7.cloned.1.call-done = f32[32,16]{1,0:T(8,128)} async-done(((f32[128,16]{1,0:T(8,128)}), f32[32,16]{1,0:T(8,128)}) %reduce-scatter.7.cloned.1.call-update) | async-done | bytes 2064
  114.0 1.7 convolution_multiply_fusion.2
  115.7 0.2 reduce-scatter.5.cloned.1.call-start
  116.0 13.4 %fusion.13 = f32[128,4096]{1,0:T(8,128)} fusion(bf16[4096,2048]{1,0:T(8,128)(2,1)} %param.17, f32[128,2048]{1,0:T(8,128)} %all-reduce.2.cloned.1.call-done, bf16[128,2048]{1,0:T(8,128)(2,1)S(1)} %copy-done.7, bf16[128,2048]{1,0:T(8,128)(2,1)S(1)} %copy-done.3), kind=kOutput, calls=%fused_computation.26 | convolution fusion | flops 2150629376 | bytes 20971520 | tf_op jit(solution)/shard_map/dot_general | solution.py:10
  129.3 12.3 %convolution_add_fusion = f32[128,4096]{1,0:T(8,128)S(1)} fusion(f32[128,4096]{1,0:T(8,128)} %fusion.13, bf16[128,2048]{1,0:T(8,128)(2,1)} %copy-done.2, bf16[4096,2048]{1,0:T(8,128)(2,1)} %param.18), kind=kOutput, calls=%fused_computation.2 | convolution fusion | flops 2148007936 | bytes 21495808 | tf_op jit(solution)/shard_map/dot_general | solution.py:10
  141.7 2.4 %fusion = f32[128,4096]{1,0:T(8,128)} fusion(f32[128,4096]{1,0:T(8,128)S(1)} %convolution_add_fusion, f32[128,16]{0,1:T(8,128)S(1)} %fusion.22, bf16[16,4096]{1,0:T(8,128)(2,1)S(1)} %copy-done.4), kind=kOutput, calls=%fused_computation.1 | convolution fusion | flops 101711872 | bytes 4333568 | tf_op jit(solution)/shard_map/dot_general | solution.py:61
  144.1 5.8 %psum.15 = bf16[128,16]{0,1:T(8,128)(2,1)S(1)} all-reduce(f32[128,16]{0,1:T(8,128)S(1)} %fusion.21), channel_id=1, replica_groups=mesh['grp'=2,'row'=4,'col'=4] {'col'}, use_global_device_ids=true, to_apply=%region_4.0 | all-reduce | flops 2048 | bytes 12288 | tf_op jit(solution)/shard_map/psum | solution.py:47
  149.9 1.6 convolution_multiply_fusion.1
  151.5 2.3 %convolution_multiply_fusion.5 = f32[16,2048]{1,0:T(8,128)} fusion(bf16[128,2048]{1,0:T(8,128)(2,1)} %param.16, bf16[128,2048]{1,0:T(8,128)(2,1)} %param.15, bf16[128,16]{0,1:T(8,128)(2,1)S(1)} %psum.15), kind=kOutput, calls=%fused_computation.9 | convolution fusion | flops 10518528 | bytes 1183744 | tf_op jit(solution)/shard_map/dot_general | solution.py:16
  153.8 1.9 fusion.2
  155.7 2.0 %reduce_sum.9 = f32[16,4096]{1,0:T(8,128)} reduce(f32[4,16,4096]{2,1,0:T(8,128)} %bitcast.24, f32[]{:T(128)} %constant.5.clone.1), dimensions={0}, to_apply=%region_3.0 | reduce | flops 196608 | bytes 1310724 | tf_op jit(solution)/shard_map/reduce_sum | solution.py:71
  157.8 29.9 %reduce-scatter.5.cloned.1.call-done = f32[32,4096]{1,0:T(8,128)} async-done(((f32[128,4096]{1,0:T(8,128)}), f32[32,4096]{1,0:T(8,128)}) %reduce-scatter.5.cloned.1.call-update) | async-done | bytes 524304 | tf_op jit(solution)/shard_map/reduce_scatter | solution.py:65
  187.6 1.8 convert_element_type.28
  (23 shorter events, 0.2 us)
Async XLA Ops:
  7.2 106.8 %copy-start = (bf16[32,4096]{1,0:T(8,128)(2,1)S(1)}, bf16[32,4096]{1,0:T(8,128)(2,1)}, u32[]{:S(2)}) copy-start(bf16[32,4096]{1,0:T(8,128)(2,1)} %param.13) | copy-start | bytes 786436
  7.2 46.5 %copy-start.5 = (bf16[16,2048]{1,0:T(8,128)(2,1)S(1)}, bf16[16,2048]{1,0:T(8,128)(2,1)}, u32[]{:S(2)}) copy-start(bf16[16,2048]{1,0:T(8,128)(2,1)} %param.22) | copy-start | bytes 196612
  7.2 83.8 %copy-start.3 = (bf16[128,2048]{1,0:T(8,128)(2,1)S(1)}, bf16[128,2048]{1,0:T(8,128)(2,1)}, u32[]{:S(2)}) copy-start(bf16[128,2048]{1,0:T(8,128)(2,1)} %param.15) | copy-start | bytes 1572868
  7.2 86.2 %copy-start.6 = (bf16[16,2048]{1,0:T(8,128)(2,1)S(1)}, bf16[16,2048]{1,0:T(8,128)(2,1)}, u32[]{:S(2)}) copy-start(bf16[16,2048]{1,0:T(8,128)(2,1)} %param.21) | copy-start | bytes 196612
  7.2 108.8 %copy-start.7 = (bf16[128,2048]{1,0:T(8,128)(2,1)S(1)}, bf16[128,2048]{1,0:T(8,128)(2,1)}, u32[]{:S(2)}) copy-start(bf16[128,2048]{1,0:T(8,128)(2,1)} %param.16) | copy-start | bytes 1572868
  7.2 33.1 %all-gather.4.cloned.1.call-start = ((), (), s32[]{:S(2)}) async-start(), calls=%async_computation.2 | async-start | bytes 1310720 | tf_op jit(solution)/shard_map/all_gather | solution.py:41
  8.0 83.1 %all-reduce.2.cloned.1.call-start = ((), (), s32[]{:S(2)}) async-start(), calls=%async_computation.3 | async-start | bytes 2097152 | tf_op jit(solution)/shard_map/psum | solution.py:47
  55.3 58.6 %reduce-scatter.7.cloned.1.call-start = ((), (), s32[]{:S(2)}) async-start(), calls=%async_computation.6 | async-start | bytes 81920
  92.5 0.8 copy-start.2
  94.4 61.3 %all-gather.6.cloned.1.call-start = ((), (), s32[]{:S(2)}) async-start(), calls=%async_computation.5 | async-start | bytes 1310720 | tf_op jit(solution)/shard_map/all_gather | solution.py:71
  115.7 26.0 %copy-start.4 = (bf16[16,4096]{1,0:T(8,128)(2,1)S(1)}, bf16[16,4096]{1,0:T(8,128)(2,1)}, u32[]{:S(2)}) copy-start(bf16[16,4096]{1,0:T(8,128)(2,1)} %param.20) | copy-start | bytes 393220
  115.7 71.9 %reduce-scatter.5.cloned.1.call-start = ((), (), s32[]{:S(2)}) async-start(), calls=%async_computation.4 | async-start | bytes 2621440 | tf_op jit(solution)/shard_map/reduce_scatter | solution.py:65
  129.3 20.6 %copy-start.1 = (bf16[128,4096]{1,0:T(8,128)(2,1)S(1)}, bf16[128,4096]{1,0:T(8,128)(2,1)}, u32[]{:S(2)}) copy-start(bf16[128,4096]{1,0:T(8,128)(2,1)} %all-gather.4.cloned.1.call-done) | copy-start | bytes 3145732
Sparse Core Ops, SparseCore 0:
  9.6 30.6 all-gather.3
  55.4 35.5 all-reduce.1
  94.5 19.4 reduce-scatter.6
  116.0 26.3 all-gather.5
  144.5 43.0 reduce-scatter.4
